TPU v7x, 32 devices: a whole 2x2x4 slice. The times are simulated.
32 devices in a mesh: row: 4 (over y, core), col: 8 (over z, x).
Axes of the slice: x: 2, y: 2, z: 4, core: 2. Of those that a mesh axis runs over, the one named last changes fastest.
Arguments:
- inverse: float32 [16384, 16384], P('row', 'col'), may hold values from -6 to 6
- front_blocks: int32 [2, 16], replicated, may hold values from 0 to 63, as said below
- panels: float32 [2, 4096, 256], P(None, 'row'), may hold values from -0.09375 to 0.09375
- diag_terms: float32 [2, 256, 256], replicated, may hold values from -6 to 6
- bounds: int32 [2, 4], replicated, may hold values from 1 to 128, 256 in all within a row
Outputs:
- border: float32 [2, 4096, 256], P(None, ('row', 'col'))
- diag_block: float32 [2, 256, 256], replicated
Inputs may be any that keep to these rules, and one draw needn't show every extreme that they name: `front_blocks`: each row names 16 distinct blocks. Positions 4 r to 4 r + 3 name blocks of four different groups of 16 consecutive blocks, and every such group is named at exactly four positions, of four different r. Positions 2 o and 2 o + 1 name blocks of two different groups of 8 consecutive blocks, and every such group is named at exactly two positions, of two different o.
All inputs are finite; a program needn't handle non-finite values.
Results may differ from a plain program's by a relative error of at most 0.0001.
Values sent between devices are 32-bit elements; how exact they have to be, the bound alone decides.
A program may use at most 128 MiB of HBM per device.

v0:
```python
import jax
import jax.numpy as jnp
from jax import lax
from jax.sharding import PartitionSpec as P

BS = 256


def body(inverse, front_blocks, panels, diag_terms, bounds):
    n_row = lax.axis_size("row")
    n_col = lax.axis_size("col")
    row_index = lax.axis_index("row")
    col_index = lax.axis_index("col")
    rows_loc, cols_loc = inverse.shape
    row_group = rows_loc // BS
    col_group = cols_loc // BS
    list_length = front_blocks.shape[1]
    per_owner = list_length // n_row
    highest = lax.Precision.HIGHEST
    borders = []
    diagonals = []
    for front_index in range(2):
        front_list = front_blocks[front_index]
        own_blocks = lax.dynamic_slice_in_dim(front_list, row_index * per_owner, per_owner)
        w_loc = panels[front_index]
        panel_width = w_loc.shape[1]
        w_pieces = w_loc.reshape(per_owner, BS, panel_width)
        targets = col_index * col_group + jnp.arange(col_group, dtype=jnp.int32)
        picker = (own_blocks[None, :] == targets[:, None]).astype(jnp.float32)
        own_piece = jnp.einsum("ki,iab->ab", picker, w_pieces, precision=highest)
        slot_rows = lax.all_gather(own_piece, "row", axis=0, tiled=True).reshape(
            n_row, BS, panel_width
        )
        owners = front_list.reshape(n_row, per_owner)
        placer = jnp.sum((owners[None, :, :] == targets[:, None, None]).astype(jnp.float32), axis=2)
        w_tilde = jnp.einsum("ks,sab->kab", placer, slot_rows, precision=highest).reshape(
            cols_loc, panel_width
        )
        dest_lists = front_list.reshape(n_row, per_owner)
        local_ids = row_index * row_group + jnp.arange(row_group, dtype=jnp.int32)
        share_rows = per_owner * BS // n_col
        full_rows = jnp.dot(inverse, w_tilde, precision=highest)
        quarters = BS // share_rows
        full_pieces = full_rows.reshape(row_group, quarters, share_rows, panel_width)
        first_rows = jnp.arange(n_col, dtype=jnp.int32) * share_rows
        dest_block = dest_lists[:, first_rows // BS]
        block_pick = (dest_block.T[:, :, None] == local_ids[None, None, :]).astype(jnp.float32)
        quarter_pick = (
            (first_rows % BS // share_rows)[:, None]
            == jnp.arange(quarters, dtype=jnp.int32)[None, :]
        ).astype(jnp.float32)
        sectioned = jnp.einsum("cq,kqap->ckap", quarter_pick, full_pieces, precision=highest)
        ordered = jnp.einsum("cdk,ckap->cdap", block_pick, sectioned, precision=highest)
        ordered = ordered.reshape(n_col * n_row * share_rows, panel_width)
        reduced = lax.psum_scatter(ordered, "col", scatter_dimension=0, tiled=True)
        received = lax.all_to_all(
            reduced.reshape(n_row, share_rows, panel_width),
            "row",
            split_axis=0,
            concat_axis=0,
            tiled=True,
        )
        product = jnp.sum(received, axis=0)
        w_mine = lax.dynamic_slice_in_dim(w_loc, col_index * share_rows, share_rows, 0)
        own_term = jnp.dot(w_mine.T, product, precision=highest)
        summed_total = lax.psum(own_term, ("row", "col"))
        node_ends = jnp.cumsum(bounds[front_index])
        columns = jnp.arange(panel_width, dtype=jnp.int32)
        node_ids = jnp.sum((columns[:, None] >= node_ends[None, :]).astype(jnp.int32), axis=1)
        same_node = (node_ids[:, None] == node_ids[None, :]).astype(jnp.float32)
        borders.append(-product)
        diagonals.append(same_node * (diag_terms[front_index] + summed_total))
    return (jnp.stack(borders), jnp.stack(diagonals))


def solution(mesh):
    placed = (P("row", "col"), P(), P(None, "row", None), P(), P())
    return jax.shard_map(
        body,
        mesh=mesh,
        in_specs=placed,
        out_specs=(P(None, ("row", "col"), None), P()),
        check_vma=False,
    )
```

profile of v0, /device:TPU:0, one launch (start us, length us, event | category | flops | bytes accessed | tf_op | source)
XLA Modules:
  0.0 484.4 jit_solution(6554460476007873666)
XLA Ops:
  7.2 0.0 all-gather.3.cloned.1.call-start
  7.2 0.8 slice_reduce_fusion.1
  8.0 1.7 fusion.46
  9.7 0.0 copy-start
  9.7 0.1 fusion.38
  9.8 0.2 convert_reduce_fusion.5
  10.0 2.3 fusion.6
  12.3 0.7 copy.51
  13.0 0.0 all-gather.3.cloned.1.call-update
  13.1 0.0 all-gather.5.cloned.1.call-start
  13.1 2.3 fusion.4
  15.5 0.7 copy.50
  16.2 0.0 all-gather.5.cloned.1.call-update
  16.2 0.0 reduce-scatter.3.cloned.1.call-start
  16.3 0.1 reshape_squeeze.12
  16.4 0.1 reshape_squeeze.14
  16.5 0.1 copy.17
  16.5 0.1 convert_reduce_fusion.1
  16.7 0.6 gather_fusion
  17.2 15.4 %all-gather.3.cloned.1.call-done = f32[1024,256]{1,0:T(8,128)} async-done(((f32[256,256]{1,0:T(8,128)}), f32[1024,256]{1,0:T(8,128)}) %all-gather.3.cloned.1.call-update) | async-done | bytes 1048592 | tf_op jit(solution)/shard_map/all_gather | solution.py:31
  32.6 4.0 fusion.10
  36.7 0.7 copy.19
  37.3 0.0 copy-done
  37.4 58.5 %convolution_bitcast_fusion.1 = f32[4096,256]{0,1:T(8,128)} fusion(f32[2048,256]{1,0:T(8,128)S(1)} %bitcast.104, f32[4096,2048]{1,0:T(8,128)} %param.5), kind=kOutput, calls=%fused_computation.7 | convolution fusion | flops 25769803776 | bytes 39845888 | tf_op jit(solution)/shard_map/dot_general | solution.py:42
  95.9 6.6 %reshape.215 = f32[16,2,128,256]{2,1,0,3:T(2,128)} reshape(f32[4096,256]{0,1:T(8,128)} %convolution_bitcast_fusion.1) | data formatting | bytes 8388608 | tf_op jit(solution)/shard_map/reshape | solution.py:44
  102.5 9.3 %copy.20 = f32[16,2,128,256]{3,1,2,0:T(2,128)} copy(f32[16,2,128,256]{2,1,0,3:T(2,128)} %reshape.215) | data formatting | bytes 8388608 | tf_op jit(solution)/shard_map/reshape | solution.py:44
  111.8 11.7 %fusion.34 = f32[8,16,128,256]{3,0,2,1:T(8,128)S(1)} fusion(f32[16,2,128,256]{3,1,2,0:T(2,128)} %copy.20, s32[8]{0:T(128)S(1)} %and_select_fusion), kind=kOutput, calls=%fused_computation.58 | convolution fusion | flops 100663312 | bytes 20971552 | tf_op jit(solution)/shard_map/cq,kqap->ckap/dot_general | solution.py:52
  123.5 12.2 %fusion.2 = f32[8,4,128,256]{3,1,2,0:T(4,128)S(1)} fusion(f32[8,16,128,256]{3,0,2,1:T(8,128)S(1)} %fusion.34, s32[16]{0:T(128)S(1)} %iota_add_fusion.1, s32[8,4]{1,0:T(8,128)S(1)} %gather_fusion), kind=kOutput, calls=%fused_computation.4 | convolution fusion | flops 201327104 | bytes 20971712 | tf_op jit(solution)/shard_map/cdk,ckap->cdap/dot_general | solution.py:53
  135.7 2.7 copy.22
  138.4 0.0 reduce-scatter.3.cloned.1.call-update
  138.4 0.0 reduce-scatter.5.cloned.1.call-start
  138.5 0.1 copy.23
  138.5 0.6 gather_fusion.1
  139.1 0.0 all-gather.5.cloned.1.call-done
  139.1 4.0 fusion.8
  143.2 0.7 copy.25
  143.8 58.8 %convolution_bitcast_fusion = f32[4096,256]{0,1:T(8,128)} fusion(f32[2048,256]{1,0:T(8,128)S(1)} %bitcast.105, f32[4096,2048]{1,0:T(8,128)} %param.5), kind=kOutput, calls=%fused_computation.6 | convolution fusion | flops 25769803776 | bytes 39845888 | tf_op jit(solution)/shard_map/dot_general | solution.py:42
  202.6 6.7 %reshape.220 = f32[16,2,128,256]{2,1,0,3:T(2,128)} reshape(f32[4096,256]{0,1:T(8,128)} %convolution_bitcast_fusion) | data formatting | bytes 8388608 | tf_op jit(solution)/shard_map/reshape | solution.py:44
  209.3 9.3 %copy.26 = f32[16,2,128,256]{3,1,2,0:T(2,128)} copy(f32[16,2,128,256]{2,1,0,3:T(2,128)} %reshape.220) | data formatting | bytes 8388608 | tf_op jit(solution)/shard_map/reshape | solution.py:44
  218.6 11.7 %fusion.32 = f32[8,16,128,256]{3,0,2,1:T(8,128)S(1)} fusion(f32[16,2,128,256]{3,1,2,0:T(2,128)} %copy.26, s32[8]{0:T(128)S(1)} %and_select_fusion), kind=kOutput, calls=%fused_computation.56 | convolution fusion | flops 100663312 | bytes 20971552 | tf_op jit(solution)/shard_map/cq,kqap->ckap/dot_general | solution.py:52
  230.3 12.2 %fusion = f32[8,4,128,256]{3,1,2,0:T(4,128)S(1)} fusion(f32[8,16,128,256]{3,0,2,1:T(8,128)S(1)} %fusion.32, s32[8,4]{1,0:T(8,128)S(1)} %gather_fusion.1, s32[16]{0:T(128)S(1)} %iota_add_fusion.1), kind=kOutput, calls=%fused_computation.2 | convolution fusion | flops 201327104 | bytes 20971712 | tf_op jit(solution)/shard_map/cdk,ckap->cdap/dot_general | solution.py:53
  242.5 2.7 copy.28
  245.2 0.0 copy-start.2
  245.2 0.0 copy-start.1
  245.2 0.0 reduce-scatter.5.cloned.1.call-update
  245.3 0.0 reduce-scatter.3.cloned.1.call-done
  245.3 3.6 all-to-all-start
  248.9 0.0 copy-done.2
  248.9 0.2 reduce-window.16
  249.1 0.2 reduce-window.17
  249.3 0.1 convert_reduce_fusion.2
  249.4 84.5 %reduce-scatter.5.cloned.1.call-done = f32[512,256]{1,0:T(8,128)} async-done(((f32[4096,256]{1,0:T(8,128)}), f32[512,256]{1,0:T(8,128)}) %reduce-scatter.5.cloned.1.call-update) | async-done | bytes 524304 | tf_op jit(solution)/shard_map/reduce_scatter | solution.py:55
  333.9 0.0 all-to-all-done
  333.9 3.5 all-to-all-start.1
  337.3 0.0 all-reduce.3.cloned.1.call-start
  337.5 2.1 fusion.18
  339.5 6.6 %all-to-all-done.1 = f32[4,128,256]{2,1,0:T(8,128)S(1)} async-done(((f32[4,128,256]{2,1,0:T(8,128)}), f32[4,128,256]{2,1,0:T(8,128)S(1)}, u32[]{:S(2)}, u32[]{:S(2)}) %all-to-all-start.1) | async-done | bytes 524320 | tf_op jit(solution)/shard_map/all_to_all | solution.py:56
  346.2 1.1 fusion.16
  347.3 0.0 all-reduce.3.cloned.1.call-update
  347.3 0.7 pad_maximum_fusion.1
  348.1 127.4 %all-reduce.3.cloned.1.call-done = (f32[256,256]{1,0:T(8,128)}, f32[256,256]{1,0:T(8,128)}) async-done(((f32[256,256]{1,0:T(8,128)}, f32[256,256]{1,0:T(8,128)}), (f32[256,256]{1,0:T(8,128)}, f32[256,256]{1,0:T(8,128)})) %all-reduce.3.cloned.1.call-update) | async-done | bytes 524304 | tf_op jit(solution)/shard_map/psum | solution.py:66
  475.5 0.0 copy-done.1
  475.5 1.2 fusion.15
  476.7 0.8 pad_maximum_fusion
  (10 shorter events, 0.1 us)
Async XLA Ops:
  7.2 25.5 %all-gather.3.cloned.1.call-start = ((), (), s32[]{:S(2)}) async-start(), calls=%async_computation.4 | async-start | bytes 1310720 | tf_op jit(solution)/shard_map/all_gather | solution.py:31
  9.7 27.7 %copy-start = (f32[1,1024,256]{2,1,0:T(8,128)}, f32[1,1024,256]{2,1,0:T(8,128)S(1)}, u32[]{:S(2)}) copy-start(f32[1,1024,256]{2,1,0:T(8,128)S(1)} %get-tuple-element.10) | copy-start | bytes 3145732
  13.1 126.1 %all-gather.5.cloned.1.call-start = ((), (), s32[]{:S(2)}) async-start(), calls=%async_computation.6 | async-start | bytes 1310720 | tf_op jit(solution)/shard_map/all_gather | solution.py:31
  16.2 229.1 %reduce-scatter.3.cloned.1.call-start = ((), (), s32[]{:S(2)}) async-start(), calls=%async_computation.5 | async-start | bytes 4718592 | tf_op jit(solution)/shard_map/reduce_scatter | solution.py:55
  138.4 195.5 %reduce-scatter.5.cloned.1.call-start = ((), (), s32[]{:S(2)}) async-start(), calls=%async_computation.7 | async-start | bytes 4718592 | tf_op jit(solution)/shard_map/reduce_scatter | solution.py:55
  245.2 3.7 copy-start.2
  245.2 230.3 %copy-start.1 = (f32[2,256,256]{2,1,0:T(8,128)S(1)}, f32[2,256,256]{2,1,0:T(8,128)}, u32[]{:S(2)}) copy-start(f32[2,256,256]{2,1,0:T(8,128)} %param.8) | copy-start | bytes 1572868
  245.3 88.6 %all-to-all-start = ((f32[4,128,256]{2,1,0:T(8,128)}), f32[4,128,256]{2,1,0:T(8,128)S(1)}, u32[]{:S(2)}, u32[]{:S(2)}) async-start(f32[4,128,256]{2,1,0:T(8,128)} %bitcast.112), calls=%async_computation.1 | async-start | bytes 1048576 | tf_op jit(solution)/shard_map/all_to_all | solution.py:56
  333.9 12.3 %all-to-all-start.1 = ((f32[4,128,256]{2,1,0:T(8,128)}), f32[4,128,256]{2,1,0:T(8,128)S(1)}, u32[]{:S(2)}, u32[]{:S(2)}) async-start(f32[4,128,256]{2,1,0:T(8,128)} %bitcast.113), calls=%async_computation.3 | async-start | bytes 1048576 | tf_op jit(solution)/shard_map/all_to_all | solution.py:56
  337.3 138.2 %all-reduce.3.cloned.1.call-start = ((), (), s32[]{:S(2)}) async-start(), calls=%async_computation.8 | async-start | bytes 1048576 | tf_op jit(solution)/shard_map/psum | solution.py:66
Sparse Core Ops, SparseCore 0:
  13.2 19.4 all-gather.2
  34.8 16.6 all-gather.4
  138.5 88.2 reduce-scatter.2
  245.4 88.4 reduce-scatter.4
  347.4 128.0 all-reduce.2
where the time goes:
time: 492 us; the launch traced here: 484 us
  waiting for transfers between devices  234 us (48%)
  matrix products  181 us (37%)
  local copies, waits for them, and re-layouts  44.1 us (9%)
  between operations  14.4 us (3%)
  starting transfers between devices  7.29 us (1%)
    psum x1, waiting for transfers between devices, body(): summed_total = lax.psum(own_term, ('row', 'col'))  127 us
    dot_general x2, matrix products, body(): full_rows = jnp.dot(inverse, w_tilde, precision=highest)  117 us
    reduce_scatter x2, waiting for transfers between devices, body(): reduced = lax.psum_scatter(ordered, 'col', scatter_dimension=0, tiled=True)  84.5 us
    reshape x4, local copies, waits for them, and re-layouts, body(): full_rows.reshape(row_group, quarters, share_rows, panel_width)  31.9 us
    dot_general x2, matrix products, body(): jnp.einsum('cdk,ckap->cdap', block_pick, sectioned, precision=highest)  24.4 us
    dot_general x2, matrix products, body(): jnp.einsum('cq,kqap->ckap', quarter_pick, full_pieces, precision=highest)  23.4 us
    all_gather x2, waiting for transfers between devices, body(): lax.all_gather(own_piece, 'row', axis=0, tiled=True)  15.4 us
  transfers between devices with their start and end apart: 7, of which 4 were waited for; matrix products, arithmetic and copies ran while one was open for 45% of the time, Pallas kernels for 0%

commit v1 on v0

--- a/solution.py
+++ b/solution.py
@@ -63,7 +63,8 @@
         product = jnp.sum(received, axis=0)
         w_mine = lax.dynamic_slice_in_dim(w_loc, col_index * share_rows, share_rows, 0)
         own_term = jnp.dot(w_mine.T, product, precision=highest)
-        summed_total = lax.psum(own_term, ("row", "col"))
+        parts = lax.all_gather(own_term, ("row", "col"), axis=0, tiled=False)
+        summed_total = parts.sum(axis=0)
         node_ends = jnp.cumsum(bounds[front_index])
         columns = jnp.arange(panel_width, dtype=jnp.int32)
         node_ids = jnp.sum((columns[:, None] >= node_ends[None, :]).astype(jnp.int32), axis=1)

time: 492 us -> 513 us (1.043)
  blocking collectives: 0 us -> 12.3 us
  other arithmetic: 3.57 us -> 10.5 us
    all_gather x0 -> x2, waiting for transfers between devices: none -> 140 us  [body(): parts = lax.all_gather(own_term, ('row', 'col'), axis=0, tiled=False)]
    psum x1 -> x0, waiting for transfers between devices: 127 us -> none  [body(): summed_total = lax.psum(own_term, ('row', 'col'))]
    all_to_all x0 -> x1, blocking collectives: none -> 12.3 us  [body(): lax.all_to_all(reduced.reshape(n_row, share_rows, panel_width), 'row', sp...]
    reduce_scatter x2, waiting for transfers between devices: 84.5 us -> 74.1 us  [body(): reduced = lax.psum_scatter(ordered, 'col', scatter_dimension=0, tiled=True)]
    reduce_sum x0 -> x2, other arithmetic: none -> 7.91 us  [body(): summed_total = parts.sum(axis=0)]
  transfers between devices with their start and end apart: 7 -> 7, of which waited for: 4 -> 5; matrix products, arithmetic and copies ran while one was open for 45% -> 45% of each run, Pallas kernels for 0% -> 0%
where the time goes in v1:
time: 513 us; the launch traced here: 505 us
  waiting for transfers between devices  238 us (46%)
  matrix products  181 us (35%)
  local copies, waits for them, and re-layouts  44.1 us (9%)
  between operations  14.8 us (3%)
  blocking collectives  12.3 us (2%)
  other arithmetic  10.5 us (2%)
    all_gather x2, waiting for transfers between devices, body(): parts = lax.all_gather(own_term, ('row', 'col'), axis=0, tiled=False)  140 us
    dot_general x2, matrix products, body(): full_rows = jnp.dot(inverse, w_tilde, precision=highest)  117 us
    reduce_scatter x2, waiting for transfers between devices, body(): reduced = lax.psum_scatter(ordered, 'col', scatter_dimension=0, tiled=True)  74.1 us
    reshape x4, local copies, waits for them, and re-layouts, body(): full_rows.reshape(row_group, quarters, share_rows, panel_width)  31.9 us
    dot_general x2, matrix products, body(): jnp.einsum('cdk,ckap->cdap', block_pick, sectioned, precision=highest)  24.4 us
    dot_general x2, matrix products, body(): jnp.einsum('cq,kqap->ckap', quarter_pick, full_pieces, precision=highest)  23.4 us
    all_gather x2, waiting for transfers between devices, body(): lax.all_gather(own_piece, 'row', axis=0, tiled=True)  15.4 us
    all_to_all x1, blocking collectives, body(): lax.all_to_all(reduced.reshape(n_row, share_rows, panel_width), 'row', sp...  12.3 us
  transfers between devices with their start and end apart: 7, of which 5 were waited for; matrix products, arithmetic and copies ran while one was open for 45% of the time, Pallas kernels for 0%

profile of v1, /device:TPU:0, one launch (start us, length us, event | category | flops | bytes accessed | tf_op | source)
XLA Modules:
  0.0 504.9 jit_solution(9402645380075751152)
XLA Ops:
  7.2 0.0 all-gather.7.cloned.1.call-start
  7.2 0.8 slice_reduce_fusion.1
  8.0 1.7 fusion.44
  9.7 0.0 copy-start
  9.7 0.1 fusion.36
  9.8 0.2 convert_reduce_fusion.5
  10.0 2.3 fusion.6
  12.3 0.7 copy.51
  13.0 0.0 all-gather.7.cloned.1.call-update
  13.1 0.0 all-gather.9.cloned.1.call-start
  13.1 2.3 fusion.4
  15.5 0.7 copy.50
  16.2 0.0 all-gather.9.cloned.1.call-update
  16.2 0.0 reduce-scatter.3.cloned.1.call-start
  16.3 0.1 reshape_squeeze.12
  16.4 0.1 reshape_squeeze.14
  16.5 0.1 copy.17
  16.5 0.1 convert_reduce_fusion.1
  16.7 0.6 gather_fusion
  17.2 15.4 %all-gather.7.cloned.1.call-done = f32[1024,256]{1,0:T(8,128)} async-done(((f32[256,256]{1,0:T(8,128)}), f32[1024,256]{1,0:T(8,128)}) %all-gather.7.cloned.1.call-update) | async-done | bytes 1048592 | tf_op jit(solution)/shard_map/all_gather | solution.py:31
  32.6 4.0 fusion.10
  36.7 0.7 copy.19
  37.4 58.5 %convolution_bitcast_fusion.1 = f32[4096,256]{0,1:T(8,128)} fusion(f32[2048,256]{1,0:T(8,128)S(1)} %bitcast.98, f32[4096,2048]{1,0:T(8,128)} %param.5), kind=kOutput, calls=%fused_computation.7 | convolution fusion | flops 25769803776 | bytes 39845888 | tf_op jit(solution)/shard_map/dot_general | solution.py:42
  95.9 6.6 %reshape.299 = f32[16,2,128,256]{2,1,0,3:T(2,128)} reshape(f32[4096,256]{0,1:T(8,128)} %convolution_bitcast_fusion.1) | data formatting | bytes 8388608 | tf_op jit(solution)/shard_map/reshape | solution.py:44
  102.5 9.3 %copy.20 = f32[16,2,128,256]{3,1,2,0:T(2,128)} copy(f32[16,2,128,256]{2,1,0,3:T(2,128)} %reshape.299) | data formatting | bytes 8388608 | tf_op jit(solution)/shard_map/reshape | solution.py:44
  111.8 11.7 %fusion.32 = f32[8,16,128,256]{3,0,2,1:T(8,128)S(1)} fusion(f32[16,2,128,256]{3,1,2,0:T(2,128)} %copy.20, s32[8]{0:T(128)S(1)} %and_select_fusion), kind=kOutput, calls=%fused_computation.56 | convolution fusion | flops 100663312 | bytes 20971552 | tf_op jit(solution)/shard_map/cq,kqap->ckap/dot_general | solution.py:52
  123.5 12.2 %fusion.2 = f32[8,4,128,256]{3,1,2,0:T(4,128)S(1)} fusion(f32[8,16,128,256]{3,0,2,1:T(8,128)S(1)} %fusion.32, s32[16]{0:T(128)S(1)} %iota_add_fusion.1, s32[8,4]{1,0:T(8,128)S(1)} %gather_fusion), kind=kOutput, calls=%fused_computation.4 | convolution fusion | flops 201327104 | bytes 20971712 | tf_op jit(solution)/shard_map/cdk,ckap->cdap/dot_general | solution.py:53
  135.7 2.7 copy.22
  138.4 0.0 reduce-scatter.3.cloned.1.call-update
  138.4 0.0 reduce-scatter.5.cloned.1.call-start
  138.5 0.1 copy.23
  138.5 0.6 gather_fusion.1
  139.1 0.0 all-gather.9.cloned.1.call-done
  139.1 4.0 fusion.8
  143.2 0.7 copy.25
  143.8 58.8 %convolution_bitcast_fusion = f32[4096,256]{0,1:T(8,128)} fusion(f32[2048,256]{1,0:T(8,128)S(1)} %bitcast.99, f32[4096,2048]{1,0:T(8,128)} %param.5), kind=kOutput, calls=%fused_computation.6 | convolution fusion | flops 25769803776 | bytes 39845888 | tf_op jit(solution)/shard_map/dot_general | solution.py:42
  202.6 6.7 %reshape.304 = f32[16,2,128,256]{2,1,0,3:T(2,128)} reshape(f32[4096,256]{0,1:T(8,128)} %convolution_bitcast_fusion) | data formatting | bytes 8388608 | tf_op jit(solution)/shard_map/reshape | solution.py:44
  209.3 9.3 %copy.26 = f32[16,2,128,256]{3,1,2,0:T(2,128)} copy(f32[16,2,128,256]{2,1,0,3:T(2,128)} %reshape.304) | data formatting | bytes 8388608 | tf_op jit(solution)/shard_map/reshape | solution.py:44
  218.6 11.7 %fusion.30 = f32[8,16,128,256]{3,0,2,1:T(8,128)S(1)} fusion(f32[16,2,128,256]{3,1,2,0:T(2,128)} %copy.26, s32[8]{0:T(128)S(1)} %and_select_fusion), kind=kOutput, calls=%fused_computation.54 | convolution fusion | flops 100663312 | bytes 20971552 | tf_op jit(solution)/shard_map/cq,kqap->ckap/dot_general | solution.py:52
  230.3 12.2 %fusion = f32[8,4,128,256]{3,1,2,0:T(4,128)S(1)} fusion(f32[8,16,128,256]{3,0,2,1:T(8,128)S(1)} %fusion.30, s32[8,4]{1,0:T(8,128)S(1)} %gather_fusion.1, s32[16]{0:T(128)S(1)} %iota_add_fusion.1), kind=kOutput, calls=%fused_computation.2 | convolution fusion | flops 201327104 | bytes 20971712 | tf_op jit(solution)/shard_map/cdk,ckap->cdap/dot_general | solution.py:53
  242.5 2.7 copy.28
  245.2 0.0 reduce-scatter.5.cloned.1.call-update
  245.3 0.0 reduce-scatter.3.cloned.1.call-done
  245.3 3.5 all-to-all-start
  248.8 0.3 all-gather.11.cloned.1.call-start
  249.1 8.5 %all-to-all-done = f32[4,128,256]{2,1,0:T(8,128)S(1)} async-done(((f32[4,128,256]{2,1,0:T(8,128)}), f32[4,128,256]{2,1,0:T(8,128)S(1)}, u32[]{:S(2)}, u32[]{:S(2)}) %all-to-all-start) | async-done | bytes 524320 | tf_op jit(solution)/shard_map/all_to_all | solution.py:56
  257.6 2.0 fusion.16
  259.6 0.0 all-gather.11.cloned.1.call-update
  259.7 0.0 all-gather.13.cloned.1.call-start
  259.7 74.1 %reduce-scatter.5.cloned.1.call-done = f32[512,256]{1,0:T(8,128)} async-done(((f32[4096,256]{1,0:T(8,128)}), f32[512,256]{1,0:T(8,128)}) %reduce-scatter.5.cloned.1.call-update) | async-done | bytes 524304 | tf_op jit(solution)/shard_map/reduce_scatter | solution.py:55
  333.8 12.3 %all_to_all.10 = f32[4,128,256]{2,1,0:T(8,128)S(1)} all-to-all(f32[4,128,256]{2,1,0:T(8,128)} %bitcast.109), channel_id=1, replica_groups=mesh['row'=4,'col'=8] {'row'}, dimensions={0} | all-to-all | bytes 1048576 | tf_op jit(solution)/shard_map/all_to_all | solution.py:56
  346.1 1.1 fusion.14
  347.2 0.0 all-gather.13.cloned.1.call-update
  347.2 0.0 copy-done.2
  347.2 0.2 reduce-window.16
  347.4 0.2 reduce-window.17
  347.6 0.1 convert_reduce_fusion.2
  347.7 0.7 pad_maximum_fusion.1
  348.4 65.6 %all-gather.11.cloned.1.call-done = f32[8192,256]{1,0:T(8,128)} async-done(((f32[256,256]{1,0:T(8,128)}), f32[8192,256]{1,0:T(8,128)}) %all-gather.11.cloned.1.call-update) | async-done | bytes 8388624 | tf_op jit(solution)/shard_map/all_gather | solution.py:66
  414.0 3.9 reduce_sum.101
  417.9 74.7 %all-gather.13.cloned.1.call-done = f32[8192,256]{1,0:T(8,128)} async-done(((f32[256,256]{1,0:T(8,128)}), f32[8192,256]{1,0:T(8,128)}) %all-gather.13.cloned.1.call-update) | async-done | bytes 8388624 | tf_op jit(solution)/shard_map/all_gather | solution.py:66
  492.6 4.0 reduce_sum.104
  496.6 0.1 fusion.13
  496.7 0.8 pad_maximum_fusion
  (14 shorter events, 0.1 us)
Async XLA Ops:
  7.2 25.5 %all-gather.7.cloned.1.call-start = ((), (), s32[]{:S(2)}) async-start(), calls=%async_computation.4 | async-start | bytes 1310720 | tf_op jit(solution)/shard_map/all_gather | solution.py:31
  9.7 27.7 %copy-start = (f32[1,1024,256]{2,1,0:T(8,128)}, f32[1,1024,256]{2,1,0:T(8,128)S(1)}, u32[]{:S(2)}) copy-start(f32[1,1024,256]{2,1,0:T(8,128)S(1)} %get-tuple-element.8) | copy-start | bytes 3145732
  13.1 126.1 %all-gather.9.cloned.1.call-start = ((), (), s32[]{:S(2)}) async-start(), calls=%async_computation.6 | async-start | bytes 1310720 | tf_op jit(solution)/shard_map/all_gather | solution.py:31
  16.2 229.1 %reduce-scatter.3.cloned.1.call-start = ((), (), s32[]{:S(2)}) async-start(), calls=%async_computation.5 | async-start | bytes 4718592 | tf_op jit(solution)/shard_map/reduce_scatter | solution.py:55
  138.4 195.4 %reduce-scatter.5.cloned.1.call-start = ((), (), s32[]{:S(2)}) async-start(), calls=%async_computation.7 | async-start | bytes 4718592 | tf_op jit(solution)/shard_map/reduce_scatter | solution.py:55
  245.2 102.0 %copy-start.2 = (s32[2,4]{1,0:T(2,128)S(1)}, s32[2,4]{1,0:T(2,128)}, u32[]{:S(2)}) copy-start(s32[2,4]{1,0:T(2,128)} %param.9) | copy-start | bytes 100
  245.3 12.3 %all-to-all-start = ((f32[4,128,256]{2,1,0:T(8,128)}), f32[4,128,256]{2,1,0:T(8,128)S(1)}, u32[]{:S(2)}, u32[]{:S(2)}) async-start(f32[4,128,256]{2,1,0:T(8,128)} %bitcast.108), calls=%async_computation.1 | async-start | bytes 1048576 | tf_op jit(solution)/shard_map/all_to_all | solution.py:56
  248.8 165.2 %all-gather.11.cloned.1.call-start = ((), (), s32[]{:S(2)}) async-start(), calls=%async_computation.8 | async-start | bytes 8650752 | tf_op jit(solution)/shard_map/all_gather | solution.py:66
  259.7 232.9 %all-gather.13.cloned.1.call-start = ((), (), s32[]{:S(2)}) async-start(), calls=%async_computation.9 | async-start | bytes 8650752 | tf_op jit(solution)/shard_map/all_gather | solution.py:66
  492.6 4.0 copy-start.1
Sparse Core Ops, SparseCore 0:
  13.2 19.4 all-gather.6
  34.8 16.6 all-gather.8
  138.5 88.2 reduce-scatter.2
  245.4 88.3 reduce-scatter.4
  337.2 76.7 all-gather.10
  416.9 75.6 all-gather.12
